TPU v7x, 32 devices: a whole 2x2x4 slice. The times are simulated.
32 devices in a mesh: subset: 4 (over x, core), slab: 8 (over z, y).
Axes of the slice: x: 2, y: 2, z: 4, core: 2. Of those that a mesh axis runs over, the one named last changes fastest.
Arguments:
- sinogram: bfloat16 [64, 64, 2048], P(('subset', 'slab')), may hold values from -12 to 12
- angles: float32 [64], P(('subset', 'slab')), may hold values from -3.140625 to 3.140625
- w_first: float32 [32, 27], replicated, may hold values from -1.25 to 1.25
- b_first: float32 [32], replicated, may hold values from -3 to 3
- w_second: float32 [32, 27], replicated, may hold values from -0.21875 to 0.21875
- b_second: float32 [1], replicated, may hold values from -3 to 3
Outputs:
- prediction: float32 [4, 32, 8, 1024], P('subset', 'slab')
- target_slab: float32 [4, 32, 8, 1024], P('subset', 'slab')
- loss: float32 [], replicated
- grad_w_first: float32 [32, 27], replicated
- grad_b_first: float32 [32], replicated
- grad_w_second: float32 [32, 27], replicated
- grad_b_second: float32 [1], replicated
All inputs are finite; a program needn't handle non-finite values.
Results may differ from a plain program's by a relative error of at most 0.00065.
The roundings to bfloat16 on the way count: a program that leaves them out, or rounds other values in their place, can miss the bound.
Values may be sent and summed in bfloat16 or wider, within the bound.
No kernel may reach another device: no remote copies, remote signals or barrier semaphores. Data moves between devices by JAX's collectives and lax.ppermute only.
A program may use at most 128 MiB of HBM per device.

v0:
```python
import functools
import math

import jax
import jax.numpy as jnp
from jax import lax
from jax.experimental import pallas as pl
from jax.experimental.pallas import tpu as pltpu
from jax.sharding import PartitionSpec as P

DET = 2048
X = 1024
Y = 8
LANES = 128
TAPS = 27
TILE = 256
BLOCK = 80
W_SECOND_AT = 32
B_SECOND_AT = 59
LOSS_AT = 64
GRAD_B_SECOND_AT = 65
HALO = 2
BOTH = ("subset", "slab")

RADIUS = math.hypot((X - 1) / 2.0, (Y - 1) / 2.0) + 0.25
FIRST_D = math.floor((DET - 1) / 2.0 - RADIUS)
LAST_D = math.floor((DET - 1) / 2.0 + RADIUS) + 1
D0 = FIRST_D // LANES * LANES
DW = -(-(LAST_D + 1 - D0) // LANES) * LANES
assert FIRST_D - D0 >= 6 and D0 + DW <= DET

F32 = jnp.float32
BF16 = jnp.bfloat16
VMEM = pl.BlockSpec(memory_space=pltpu.VMEM)
SMEM = pl.BlockSpec(memory_space=pltpu.SMEM)


def iota(shape, dim):
    return lax.broadcasted_iota(jnp.int32, shape, dim)


def split2(value):
    high = value.astype(BF16)
    return high, (value - high.astype(F32)).astype(BF16)


def dot(a, b):
    return jnp.dot(a, b, preferred_element_type=F32)


def dot_nt(a, b):
    return lax.dot_general(a, b, (((1,), (1,)), ((), ())), preferred_element_type=F32)


def pack_kernel(depth, trig_ref, sino_ref, out_ref, rows_ref):
    views, z_count = sino_ref.shape[0], sino_ref.shape[1]
    rows = depth + 2 * HALO
    lane = iota((rows, LANES), 1)
    zeros = jnp.zeros((8, DW), F32)
    for view in range(views):
        rows_ref[0:8, :] = zeros
        rows_ref[8 : 8 + z_count, :] = sino_ref[view, :, D0 : D0 + DW].astype(F32)
        rows_ref[8 + z_count : 16 + z_count, :] = zeros
        head = jnp.zeros((rows, LANES), F32)
        for which in range(2):
            left = jnp.full((rows, LANES), trig_ref[which, view], F32)
            for part in range(3):
                piece = left.astype(BF16).astype(F32)
                left = left - piece
                head = jnp.where(lane == 3 * which + part, piece, head)
        for to in range(out_ref.shape[0]):
            start = 8 + to * depth - HALO
            out_ref[to, view] = rows_ref[start : start + rows, :].astype(BF16)
            first = rows_ref[start : start + rows, 0:LANES]
            out_ref[to, view, :, 0:LANES] = jnp.where(lane < 6, head, first).astype(BF16)


def pack(trig, sino, group, depth):
    views, z_count = sino.shape[0], sino.shape[1]
    return pl.pallas_call(
        functools.partial(pack_kernel, depth),
        out_shape=jax.ShapeDtypeStruct((group, views, depth + 2 * HALO, DW), BF16),
        in_specs=[SMEM, VMEM],
        out_specs=VMEM,
        scratch_shapes=[pltpu.VMEM((z_count + 16, DW), F32)],
        name="pack",
    )(trig, sino)


def project_kernel(scale, data_ref, ext_ref, own_ref, low_ref, high_ref, tab_ref, scal_ref, sem):
    views, rows = data_ref.shape[0], data_ref.shape[1]
    centre = (DET - 1) / 2.0
    head = data_ref[:, 0, 0:LANES].astype(F32)
    cosine = jnp.broadcast_to(head[:, 0:1] + head[:, 1:2] + head[:, 2:3], (views, LANES))
    sine = jnp.broadcast_to(head[:, 3:4] + head[:, 4:5] + head[:, 5:6], (views, LANES))

    def at(col, row):
        return col * cosine + row * sine + centre

    start = (iota((views, LANES), 1) % (X // LANES)).astype(F32) * LANES - (X - 1) / 2.0
    stop = start + (LANES - 1.0)
    edge = (Y - 1) / 2.0
    least = jnp.minimum(
        jnp.minimum(at(start, -edge), at(stop, -edge)), jnp.minimum(at(start, edge), at(stop, edge))
    )
    tab_ref[0] = cosine
    tab_ref[1] = sine
    tab_ref[2] = ((jnp.floor(least).astype(jnp.int32) - D0) // LANES).astype(F32)
    copy = pltpu.make_async_copy(tab_ref, scal_ref, sem)
    copy.start()
    values = data_ref[...].astype(F32)
    low_ref[...] = values
    high_ref[...] = pltpu.roll(values.reshape(views * rows, DW), DW - 1, 1).reshape(values.shape)
    copy.wait()

    column = iota((Y, LANES), 1).astype(F32)
    row_pos = iota((Y, LANES), 0).astype(F32) - edge

    for block in range(X // LANES):
        col = column + (block * LANES - (X - 1) / 2.0)

        def one_view(view, sums):
            tile = scal_ref[2, view, block].astype(jnp.int32)
            position = col * scal_ref[0, view, 0] + row_pos * scal_ref[1, view, 0] + centre
            lower = jnp.floor(position)
            weight_low = jnp.maximum(0.0, 1.0 - jnp.abs(position - lower))
            weight_high = jnp.maximum(0.0, 1.0 - jnp.abs(position - (lower + 1.0)))
            weight_low = weight_low.astype(BF16).astype(F32)
            weight_high = weight_high.astype(BF16).astype(F32)
            index = lower.astype(jnp.int32) - (D0 + tile * LANES)
            second = index >= LANES
            index = jnp.bitwise_and(index, LANES - 1)
            offset = pl.multiple_of(tile * LANES, LANES)

            def take(ref, z):
                def part(at_lane):
                    line = jnp.broadcast_to(
                        ref[view, z : z + 1, pl.ds(at_lane, LANES)], (Y, LANES)
                    )
                    return jnp.take_along_axis(line, index, axis=1, mode="promise_in_bounds")

                return jnp.where(second, part(offset + LANES), part(offset))

            return tuple(
                sums[z] + (weight_low * take(low_ref, z) + weight_high * take(high_ref, z))
                for z in range(rows)
            )

        empty = tuple(jnp.zeros((Y, LANES), F32) for _ in range(rows))
        sums = lax.fori_loop(0, views, one_view, empty, unroll=8)
        for z in range(rows):
            done = sums[z] * scale
            ext_ref[z, :, block * LANES : (block + 1) * LANES] = done
            if HALO <= z < rows - HALO:
                own_ref[z - HALO, :, block * LANES : (block + 1) * LANES] = done


def project(data, scale):
    views, rows = data.shape[0], data.shape[1]
    return pl.pallas_call(
        functools.partial(project_kernel, scale),
        out_shape=(
            jax.ShapeDtypeStruct((rows, Y, X), F32),
            jax.ShapeDtypeStruct((rows - 2 * HALO, Y, X), F32),
        ),
        in_specs=[VMEM],
        out_specs=(VMEM, VMEM),
        scratch_shapes=[
            pltpu.VMEM((views, rows, DW), F32),
            pltpu.VMEM((views, rows, DW), F32),
            pltpu.VMEM((3, views, LANES), F32),
            pltpu.SMEM((3, views, LANES), F32),
            pltpu.SemaphoreType.DMA,
        ],
        name="project",
    )(data)


def select_taps(shape, rows_first, dy, column_of):
    param = iota(shape, 0 if rows_first else 1)
    row = iota(shape, 1 if rows_first else 0)
    row = row % BLOCK
    return param, row, column_of(row // 24, (row // 8) % 3, dy)


def first_column(dx, dz, dy):
    return 9 * dz + 3 * dy + dx


def second_column(dx, dz, dy):
    return W_SECOND_AT + (TAPS - 1) - first_column(dx, dz, dy)


def spread(params, column_of, bias):
    channels = params.shape[0]
    height = channels * Y
    high, low = split2(params)
    both = jnp.concatenate([high, low], axis=1)
    rep = (iota((height, channels), 0) // Y == iota((height, channels), 1)).astype(F32)
    rep = rep.astype(BF16)
    shape = (2 * LANES, TILE)
    source = iota(shape, 0)
    col = iota(shape, 1)
    part, inner = col // BLOCK, col % BLOCK
    wanted_half = jnp.where(part == 2, 1, 0)
    usable = (part < 3) & (source // LANES == wanted_half)
    out_col = iota((height, TILE), 1)
    out_inner = out_col % BLOCK
    out_y = iota((height, TILE), 0) % Y
    total = jnp.zeros((height, TILE), F32)
    for dy in range(3):
        wanted = column_of(inner // 24, (inner // 8) % 3, dy)
        pick = usable & (inner < 72) & (source % LANES == wanted)
        if bias and dy == 1:
            pick = pick | (usable & (inner == 72) & (source % LANES == TAPS))
        chosen = dot(both, pick.astype(F32).astype(BF16)).astype(BF16)
        here = (out_inner < 72) & (out_inner % 8 - out_y + 1 == dy)
        if bias and dy == 1:
            here = here | (out_inner == 72)
        total = total + jnp.where(here, dot(rep, chosen), 0.0)
    return total.astype(BF16)


def gather_taps(grad, channels, column_of, bias):
    height = channels * Y
    rep = (iota((channels, height), 1) // Y == iota((channels, height), 0)).astype(F32)
    col = iota((height, BLOCK), 1)
    row_y = iota((height, BLOCK), 0) % Y
    inner = iota((BLOCK, LANES), 0)
    to = iota((BLOCK, LANES), 1)
    total = jnp.zeros((channels, LANES), F32)
    for dy in range(3):
        here = (col < 72) & (col % 8 - row_y + 1 == dy)
        pick = (inner < 72) & (to == column_of(inner // 24, (inner // 8) % 3, dy))
        if bias and dy == 1:
            here = here | (col == 72)
            pick = pick | ((inner == 72) & (to == TAPS))
        summed = jnp.dot(
            rep,
            jnp.where(here, grad, 0.0),
            precision=lax.Precision.HIGHEST,
            preferred_element_type=F32,
        )
        total = total + jnp.dot(
            summed,
            pick.astype(F32),
            precision=lax.Precision.HIGHEST,
            preferred_element_type=F32,
        )
    return total


def shift_columns(value, by):
    if by == 0:
        return value
    rolled = pltpu.roll(value, (-by) % X, 1)
    lane = iota(value.shape, 1)
    return jnp.where(lane == (X - 1 if by > 0 else 0), 0.0, rolled)


def fill_shifted(ref, field):
    for dx in range(3):
        ref[dx] = shift_columns(field, dx - 1)


def patch(ref, slice_index, tile):
    at = pl.multiple_of(slice_index * Y, Y)
    cols = slice(tile * TILE, (tile + 1) * TILE)
    pieces = [ref[dx, pl.ds(at, 3 * Y), cols] for dx in range(3)]
    pieces.append((iota((8, TILE), 0) == 0).astype(F32))
    high, low = split2(jnp.concatenate(pieces, axis=0))
    return high, low


def apply_spread(weights, high, low):
    return dot(weights[:, 0 : 3 * BLOCK], jnp.concatenate([high, low, high], axis=0))


def slice_flag(hidden_slice, hidden_count):
    n_slab = lax.axis_size("slab")
    place = (lax.axis_index("subset") % 2) * n_slab + lax.axis_index("slab")
    outside = ((hidden_slice == 0) & (place == 0)) | (
        (hidden_slice == hidden_count - 1) & (place == 2 * n_slab - 1)
    )
    return jnp.where(outside, 0.0, 1.0).astype(F32)


def forward_kernel(ext_ref, params_ref, pred_ref, first_ref, second_ref, shifted_ref, acc_ref):
    rows = ext_ref.shape[0]
    hidden_count = rows - 2
    params = params_ref[...]
    first = spread(params, first_column, True)
    second = spread(params, second_column, False)
    first_ref[...] = first
    second_ref[...] = second
    second_t = second.astype(F32).T.astype(BF16)
    fill_shifted(shifted_ref, ext_ref[...].reshape(rows * Y, X))
    acc_ref[...] = jnp.zeros(acc_ref.shape, F32)

    def one_slice(hidden_slice, carry):
        flag = slice_flag(hidden_slice, hidden_count)
        at = pl.multiple_of(hidden_slice * Y, Y)
        for tile in range(X // TILE):
            cols = slice(tile * TILE, (tile + 1) * TILE)
            high, low = patch(shifted_ref, hidden_slice, tile)
            hidden = jnp.maximum(apply_spread(first, high, low), 0.0) * flag
            h_high, h_low = split2(hidden)
            main = dot(second_t[BLOCK : 3 * BLOCK], h_high)
            taps = main[0:BLOCK] + main[BLOCK : 2 * BLOCK] + dot(second_t[0:BLOCK], h_low)
            for dx in range(3):
                acc_ref[dx, pl.ds(at, 3 * Y), cols] += taps[24 * dx : 24 * dx + 24]
        return carry

    lax.fori_loop(0, hidden_count, one_slice, 0)
    inner = slice(HALO * Y, (rows - HALO) * Y)
    added = acc_ref[1, inner, :]
    for dx in (0, 2):
        added = added + shift_columns(acc_ref[dx, inner, :], 1 - dx)
    own = ext_ref[HALO : rows - HALO].reshape(added.shape)
    bias = params[0:1, B_SECOND_AT : B_SECOND_AT + 1]
    pred_ref[...] = (own + added + bias).reshape(pred_ref.shape)


def forward(ext, params):
    rows = ext.shape[0]
    height = params.shape[0] * Y
    return pl.pallas_call(
        forward_kernel,
        out_shape=(
            jax.ShapeDtypeStruct((rows - 2 * HALO, Y, X), F32),
            jax.ShapeDtypeStruct((height, TILE), BF16),
            jax.ShapeDtypeStruct((height, TILE), BF16),
        ),
        in_specs=[VMEM, VMEM],
        out_specs=(VMEM, VMEM, VMEM),
        scratch_shapes=[
            pltpu.VMEM((3, rows * Y, X), F32),
            pltpu.VMEM((3, rows * Y, X), F32),
        ],
        cost_estimate=pl.CostEstimate(
            flops=20_000_000_000, bytes_accessed=2_000_000, transcendentals=0
        ),
        name="forward",
    )(ext, params)


def backward_kernel(
    cells,
    ext_ref,
    pred_ref,
    target_ref,
    first_ref,
    second_ref,
    out_ref,
    shifted_ref,
    grad_ref,
    acc1_ref,
    acc2_ref,
):
    rows = ext_ref.shape[0]
    hidden_count = rows - 2
    height = first_ref.shape[0]
    channels = height // Y
    diff = (pred_ref[...] - target_ref[...]).reshape((rows - 2 * HALO) * Y, X)
    resid = 2.0 * diff / cells
    loss = jnp.sum(diff * diff, keepdims=True) / cells
    grad_b2 = jnp.sum(resid, keepdims=True)
    fill_shifted(shifted_ref, ext_ref[...].reshape(rows * Y, X))
    inner = slice(HALO * Y, (rows - HALO) * Y)
    for dx in range(3):
        grad_ref[dx, 0 : HALO * Y, :] = jnp.zeros((HALO * Y, X), F32)
        grad_ref[dx, (rows - HALO) * Y : rows * Y, :] = jnp.zeros((HALO * Y, X), F32)
        grad_ref[dx, inner, :] = shift_columns(resid, dx - 1)
    acc1_ref[...] = jnp.zeros(acc1_ref.shape, F32)
    acc2_ref[...] = jnp.zeros(acc2_ref.shape, F32)
    first = first_ref[...]
    second = second_ref[...]

    def one_slice(hidden_slice, carry):
        flag = slice_flag(hidden_slice, hidden_count)
        sum1 = None
        sum2 = None
        for tile in range(X // TILE):
            high, low = patch(shifted_ref, hidden_slice, tile)
            g_high, g_low = patch(grad_ref, hidden_slice, tile)
            hidden = jnp.maximum(apply_spread(first, high, low), 0.0) * flag
            grad_pre = jnp.where(hidden > 0.0, apply_spread(second, g_high, g_low), 0.0)
            part1 = dot_nt(
                jnp.concatenate(split2(grad_pre), axis=0), jnp.concatenate([high, low], axis=0)
            )
            part2 = dot_nt(
                jnp.concatenate(split2(hidden), axis=0), jnp.concatenate([g_high, g_low], axis=0)
            )
            sum1 = part1 if sum1 is None else sum1 + part1
            sum2 = part2 if sum2 is None else sum2 + part2
        acc1_ref[...] += sum1
        acc2_ref[...] += sum2
        return carry

    lax.fori_loop(0, hidden_count, one_slice, 0)

    def folded(ref):
        value = ref[...]
        value = value[0:height] + value[height : 2 * height]
        return value[:, 0:BLOCK] + value[:, BLOCK : 2 * BLOCK]

    total = gather_taps(folded(acc1_ref), channels, first_column, True)
    total = total + gather_taps(folded(acc2_ref), channels, second_column, False)
    lane = iota(total.shape, 1)
    row = iota(total.shape, 0)
    total = jnp.where((row == 0) & (lane == LOSS_AT), loss, total)
    total = jnp.where((row == 0) & (lane == GRAD_B_SECOND_AT), grad_b2, total)
    out_ref[...] = total


def backward(ext, pred, target, first, second, cells):
    rows = ext.shape[0]
    height = first.shape[0]
    return pl.pallas_call(
        functools.partial(backward_kernel, cells),
        out_shape=jax.ShapeDtypeStruct((height // Y, LANES), F32),
        in_specs=[VMEM] * 5,
        out_specs=VMEM,
        scratch_shapes=[
            pltpu.VMEM((3, rows * Y, X), F32),
            pltpu.VMEM((3, rows * Y, X), F32),
            pltpu.VMEM((2 * height, 2 * BLOCK), F32),
            pltpu.VMEM((2 * height, 2 * BLOCK), F32),
        ],
        name="backward",
    )(ext, pred, target, first, second)


def sum_everywhere(value):
    devices = lax.axis_size("subset") * lax.axis_size("slab")
    apart = 1
    while apart < devices:
        pairs = [(i, i ^ apart) for i in range(devices)]
        value = value + lax.ppermute(value, BOTH, pairs)
        apart *= 2
    return value


def body(sinogram, angles, w_first, b_first, w_second, b_second):
    n_sub = lax.axis_size("subset") // 2
    n_slab = lax.axis_size("slab")
    devices = 2 * n_sub * n_slab
    group = 2 * n_slab
    local_views, z_count = sinogram.shape[0], sinogram.shape[1]
    depth = z_count // group
    channels = w_first.shape[0]
    scale = math.pi / (local_views * group)
    cells = float(n_sub * z_count * Y * X)
    assert devices & (devices - 1) == 0 and channels == 32 and depth >= HALO

    trig = jnp.stack([jnp.cos(angles), jnp.sin(angles)])
    params = jnp.concatenate(
        [
            w_first,
            b_first[:, None],
            jnp.zeros((channels, W_SECOND_AT - TAPS - 1), F32),
            w_second,
            jnp.broadcast_to(b_second, (channels, LANES - W_SECOND_AT - TAPS)),
        ],
        axis=1,
    )
    sent = pack(trig, sinogram, group, depth)
    groups = [list(range(s * group, (s + 1) * group)) for s in range(n_sub)]
    got = lax.all_to_all(sent, BOTH, 0, 0, axis_index_groups=groups)
    got = got.reshape(group * local_views, depth + 2 * HALO, DW)
    ext, own = project(got, scale)

    others = None
    for apart in range(1, n_sub):
        pairs = [(i, (i + apart * group) % devices) for i in range(devices)]
        arrived = lax.ppermute(own, BOTH, pairs)
        others = arrived if others is None else others + arrived
    target = others if n_sub == 2 else others / (n_sub - 1)

    pred, first, second = forward(ext, params)
    partial = backward(ext, pred, target, first, second, cells)
    total = sum_everywhere(partial)
    return (
        pred[None],
        target[None],
        total[0, LOSS_AT],
        total[:, 0:TAPS],
        total[:, TAPS],
        total[:, W_SECOND_AT : W_SECOND_AT + TAPS],
        total[0, GRAD_B_SECOND_AT : GRAD_B_SECOND_AT + 1],
    )


def solution(mesh):
    return jax.shard_map(
        body,
        mesh=mesh,
        in_specs=(P(BOTH, None, None), P(BOTH), P(), P(), P(), P()),
        out_specs=(
            P("subset", "slab", None, None),
            P("subset", "slab", None, None),
            P(),
            P(),
            P(),
            P(),
            P(),
        ),
        check_vma=False,
    )
```

profile of v0, /device:TPU:0, one launch (start us, length us, event | category | flops | bytes accessed | tf_op | source)
XLA Modules:
  0.0 86.4 jit_solution(14874565309462313472)
XLA Ops:
  0.6 0.7 cosine_bitcast_fusion
  1.3 0.6 pad_maximum_fusion.trig_ref
  1.9 2.1 %pack.1 = bf16[16,2,8,1280]{3,2,1,0:T(8,128)(2,1)} custom-call(f32[2,2]{1,0:T(2,128)} %pad_maximum_fusion.trig_ref, bf16[2,64,2048]{2,1,0:T(8,128)(2,1)} %sino_ref.1), custom_call_target="tpu_custom_call" | custom-call | tf_op jit(solution)/shard_map/pack/pallas_call | solution.py:80
  4.0 7.4 %all-to-all-start = ((bf16[16,2,8,1280]{3,2,1,0:T(8,128)(2,1)}), bf16[16,2,8,1280]{3,2,1,0:T(8,128)(2,1)S(1)}, u32[]{:S(2)}, u32[]{:S(2)}) async-start(bf16[16,2,8,1280]{3,2,1,0:T(8,128)(2,1)} %pack.1), calls=%async_computation | async-start | bytes 1310720 | tf_op jit(solution)/shard_map/all_to_all | solution.py:469
  12.1 0.0 copy-start.5
  12.1 0.6 copy-done.5
  12.8 0.1 copy.14
  12.9 0.0 copy-start.3
  12.9 0.0 copy-start.4
  12.9 0.7 copy-done.3
  13.6 0.0 copy-done.4
  13.6 0.7 concatenate.3.params_ref
  14.3 15.7 %all-to-all-done = bf16[16,2,8,1280]{3,2,1,0:T(8,128)(2,1)S(1)} async-done(((bf16[16,2,8,1280]{3,2,1,0:T(8,128)(2,1)}), bf16[16,2,8,1280]{3,2,1,0:T(8,128)(2,1)S(1)}, u32[]{:S(2)}, u32[]{:S(2)}) %all-to-all-start) | async-done | bytes 655392 | tf_op jit(solution)/shard_map/all_to_all | solution.py:469
  30.0 0.0 copy-start
  30.0 0.8 copy-done
  30.8 15.5 %project.1 = (f32[8,8,1024]{2,1,0:T(8,128)}, f32[4,8,1024]{2,1,0:T(8,128)}) custom-call(bf16[32,8,1280]{2,1,0:T(8,128)(2,1)} %bitcast.12), custom_call_target="tpu_custom_call" | custom-call | tf_op jit(solution)/shard_map/project/pallas_call | solution.py:160
  46.3 1.6 %collective-permute-start = (f32[4,8,1024]{2,1,0:T(8,128)}, f32[4,8,1024]{2,1,0:T(8,128)S(1)}, u32[]{:S(2)}, u32[]{:S(2)}) collective-permute-start(f32[4,8,1024]{2,1,0:T(8,128)} %get-tuple-element.14), channel_id=1, source_target_pairs={{0,16},{1,17},{2,18},{3,19},{4,20},{5,21},{6,22},{7,23},{8,24},{9,... | collective-permute-start | bytes 393224 | tf_op jit(solution)/shard_map/ppermute | solution.py:476
  47.9 6.6 %forward.1 = (f32[4,8,1024]{2,1,0:T(8,128)}, bf16[256,256]{1,0:T(8,128)(2,1)}, bf16[256,256]{1,0:T(8,128)(2,1)}) custom-call(f32[8,8,1024]{2,1,0:T(8,128)} %get-tuple-element.12.ext_ref, f32[32,128]{1,0:T(8,128)} %concatenate.3.params_ref), custom_call_target="tpu_custom_call" | custom-call | flops 20000000000 | bytes 2000000 | tf_op jit(solution)/shard_map/forward/pallas_call | solution.py:327
  54.4 0.0 collective-permute-done.target_ref
  54.4 0.0 copy-start.1
  54.4 0.7 copy-done.1
  55.1 10.6 %backward.1 = f32[32,128]{1,0:T(8,128)} custom-call(f32[8,8,1024]{2,1,0:T(8,128)} %get-tuple-element.12.ext_ref, f32[4,8,1024]{2,1,0:T(8,128)} %get-tuple-element.13.pred_ref, f32[4,8,1024]{2,1,0:T(8,128)} %copy-done.1, bf16[256,256]{1,0:T(8,128)(2,1)} %get-tuple-element.15.first_ref, bf16[256,256]{1,0:T(8,128)(2,1)} %get-tuple-element.16.second_ref), custom_call_target="tpu_custom_call" | custom-call | tf_op jit(solution)/shard_map/backward/pallas_call | solution.py:419
  65.7 0.6 collective-permute-start.1
  66.3 3.4 %collective-permute-done.1 = f32[32,128]{1,0:T(8,128)S(1)} collective-permute-done((f32[32,128]{1,0:T(8,128)}, f32[32,128]{1,0:T(8,128)S(1)}, u32[]{:S(2)}, u32[]{:S(2)}) %collective-permute-start.1) | collective-permute-done | bytes 16416 | tf_op jit(solution)/shard_map/ppermute | solution.py:439
  69.7 0.7 add.15
  70.4 1.0 %collective-permute-start.2 = (f32[32,128]{1,0:T(8,128)S(1)}, f32[32,128]{1,0:T(8,128)S(1)}, u32[]{:S(2)}, u32[]{:S(2)}) collective-permute-start(f32[32,128]{1,0:T(8,128)S(1)} %add.15), channel_id=1, source_target_pairs={{0,2},{1,3},{2,0},{3,1},{4,6},{5,7},{6,4},{7,5},{8,10},{9,11},{10,... | collective-permute-start | bytes 49160 | tf_op jit(solution)/shard_map/ppermute | solution.py:439
  71.4 2.8 %collective-permute-done.2 = f32[32,128]{1,0:T(8,128)S(1)} collective-permute-done((f32[32,128]{1,0:T(8,128)S(1)}, f32[32,128]{1,0:T(8,128)S(1)}, u32[]{:S(2)}, u32[]{:S(2)}) %collective-permute-start.2) | collective-permute-done | bytes 16416 | tf_op jit(solution)/shard_map/ppermute | solution.py:439
  74.2 0.0 copy-start.2
  74.2 0.0 collective-permute-start.3
  74.2 4.6 %collective-permute-done.3 = f32[32,128]{1,0:T(8,128)S(1)} collective-permute-done((f32[32,128]{1,0:T(8,128)S(1)}, f32[32,128]{1,0:T(8,128)S(1)}, u32[]{:S(2)}, u32[]{:S(2)}) %collective-permute-start.3) | collective-permute-done | bytes 16416 | tf_op jit(solution)/shard_map/ppermute | solution.py:439
  78.9 0.0 collective-permute-start.4
  78.9 1.2 %collective-permute-done.4 = f32[32,128]{1,0:T(8,128)S(1)} collective-permute-done((f32[32,128]{1,0:T(8,128)S(1)}, f32[32,128]{1,0:T(8,128)S(1)}, u32[]{:S(2)}, u32[]{:S(2)}) %collective-permute-start.4) | collective-permute-done | bytes 16416 | tf_op jit(solution)/shard_map/ppermute | solution.py:439
  80.0 0.5 collective-permute-start.5
  80.6 3.2 %collective-permute-done.5 = f32[32,128]{1,0:T(8,128)S(1)} collective-permute-done((f32[32,128]{1,0:T(8,128)S(1)}, f32[32,128]{1,0:T(8,128)S(1)}, u32[]{:S(2)}, u32[]{:S(2)}) %collective-permute-start.5) | collective-permute-done | bytes 16416 | tf_op jit(solution)/shard_map/ppermute | solution.py:439
  83.8 0.7 fusion.1
  84.5 0.6 fusion
  85.1 0.7 slice_reduce_fusion
  85.7 0.0 copy-done.2
  85.8 0.7 copy.17
  (6 shorter events, 0.0 us)
Async XLA Ops:
  4.0 25.9 %all-to-all-start = ((bf16[16,2,8,1280]{3,2,1,0:T(8,128)(2,1)}), bf16[16,2,8,1280]{3,2,1,0:T(8,128)(2,1)S(1)}, u32[]{:S(2)}, u32[]{:S(2)}) async-start(bf16[16,2,8,1280]{3,2,1,0:T(8,128)(2,1)} %pack.1), calls=%async_computation | async-start | bytes 1310720 | tf_op jit(solution)/shard_map/all_to_all | solution.py:469
  12.1 0.7 copy-start.5
  12.9 0.7 copy-start.3
  12.9 0.7 copy-start.4
  30.0 0.8 copy-start
  46.3 8.1 %collective-permute-start = (f32[4,8,1024]{2,1,0:T(8,128)}, f32[4,8,1024]{2,1,0:T(8,128)S(1)}, u32[]{:S(2)}, u32[]{:S(2)}) collective-permute-start(f32[4,8,1024]{2,1,0:T(8,128)} %get-tuple-element.14), channel_id=1, source_target_pairs={{0,16},{1,17},{2,18},{3,19},{4,20},{5,21},{6,22},{7,23},{8,24},{9,... | collective-permute-start | bytes 393224 | tf_op jit(solution)/shard_map/ppermute | solution.py:476
  54.4 0.7 copy-start.1
  65.7 3.9 %collective-permute-start.1 = (f32[32,128]{1,0:T(8,128)}, f32[32,128]{1,0:T(8,128)S(1)}, u32[]{:S(2)}, u32[]{:S(2)}) collective-permute-start(f32[32,128]{1,0:T(8,128)} %backward.1), channel_id=1, source_target_pairs={{0,1},{1,0},{2,3},{3,2},{4,5},{5,4},{6,7},{7,6},{8,9},{9,8},{10,11... | collective-permute-start | bytes 49160 | tf_op jit(solution)/shard_map/ppermute | solution.py:439
  70.4 3.8 %collective-permute-start.2 = (f32[32,128]{1,0:T(8,128)S(1)}, f32[32,128]{1,0:T(8,128)S(1)}, u32[]{:S(2)}, u32[]{:S(2)}) collective-permute-start(f32[32,128]{1,0:T(8,128)S(1)} %add.15), channel_id=1, source_target_pairs={{0,2},{1,3},{2,0},{3,1},{4,6},{5,7},{6,4},{7,5},{8,10},{9,11},{10,... | collective-permute-start | bytes 49160 | tf_op jit(solution)/shard_map/ppermute | solution.py:439
  74.2 11.5 %copy-start.2 = (f32[4,8,1024]{2,1,0:T(8,128)S(1)}, f32[4,8,1024]{2,1,0:T(8,128)}, u32[]{:S(2)}) copy-start(f32[4,8,1024]{2,1,0:T(8,128)} %copy-done.1) | copy-start | bytes 393220
  74.2 4.6 %collective-permute-start.3 = (f32[32,128]{1,0:T(8,128)S(1)}, f32[32,128]{1,0:T(8,128)S(1)}, u32[]{:S(2)}, u32[]{:S(2)}) collective-permute-start(f32[32,128]{1,0:T(8,128)S(1)} %add.16), channel_id=1, source_target_pairs={{0,4},{1,5},{2,6},{3,7},{4,0},{5,1},{6,2},{7,3},{8,12},{9,13},{10,... | collective-permute-start | bytes 49160 | tf_op jit(solution)/shard_map/ppermute | solution.py:439
  78.9 1.2 %collective-permute-start.4 = (f32[32,128]{1,0:T(8,128)S(1)}, f32[32,128]{1,0:T(8,128)S(1)}, u32[]{:S(2)}, u32[]{:S(2)}) collective-permute-start(f32[32,128]{1,0:T(8,128)S(1)} %add.17), channel_id=1, source_target_pairs={{0,8},{1,9},{2,10},{3,11},{4,12},{5,13},{6,14},{7,15},{8,0},{9,1},... | collective-permute-start | bytes 49160 | tf_op jit(solution)/shard_map/ppermute | solution.py:439
  80.0 3.7 %collective-permute-start.5 = (f32[32,128]{1,0:T(8,128)S(1)}, f32[32,128]{1,0:T(8,128)S(1)}, u32[]{:S(2)}, u32[]{:S(2)}) collective-permute-start(f32[32,128]{1,0:T(8,128)S(1)} %add.18), channel_id=1, source_target_pairs={{0,16},{1,17},{2,18},{3,19},{4,20},{5,21},{6,22},{7,23},{8,24},{9,... | collective-permute-start | bytes 49160 | tf_op jit(solution)/shard_map/ppermute | solution.py:439
where the time goes:
time: 86.9 us; the launch traced here: 86.4 us
  Pallas kernels  34.8 us (40%)
  waiting for transfers between devices  30.9 us (36%)
  starting transfers between devices  11.1 us (13%)
  local copies, waits for them, and re-layouts  6.97 us (8%)
  between operations  1.34 us (2%)
  other arithmetic  1.31 us (2%)
    all_to_all x1, waiting for transfers between devices, body(): got = lax.all_to_all(sent, BOTH, 0, 0, axis_index_groups=groups)  15.7 us
    pallas_call x1, Pallas kernels, project(): pl.pallas_call(functools.partial(project_kernel, scale), out_shape=(jax.S...  15.5 us
    ppermute x5, waiting for transfers between devices, sum_everywhere(): value = value + lax.ppermute(value, BOTH, pairs)  15.2 us
    pallas_call x1, Pallas kernels, backward(): pl.pallas_call(functools.partial(backward_kernel, cells), out_shape=jax.S...  10.6 us
    all_to_all x1, starting transfers between devices, body(): got = lax.all_to_all(sent, BOTH, 0, 0, axis_index_groups=groups)  7.41 us
    pallas_call x1, Pallas kernels, forward(): pl.pallas_call(forward_kernel, out_shape=(jax.ShapeDtypeStruct((rows - 2...  6.57 us
    unnamed x13, local copies, waits for them, and re-layouts  3.53 us
    pallas_call x1, Pallas kernels, pack(): pl.pallas_call(functools.partial(pack_kernel, depth), out_shape=jax.Shape...  2.13 us
  transfers between devices with their start and end apart: 7, of which 6 were waited for; matrix products, arithmetic and copies ran while one was open for 1% of the time, Pallas kernels for 8%

commit v1 on v0

--- a/solution.py
+++ b/solution.py
@@ -35,6 +35,10 @@
 SMEM = pl.BlockSpec(memory_space=pltpu.SMEM)
 
 
+def vmem_mib(count):
+    return pltpu.CompilerParams(vmem_limit_bytes=count * 2**20)
+
+
 def iota(shape, dim):
     return lax.broadcasted_iota(jnp.int32, shape, dim)
 
@@ -52,7 +56,7 @@
     return lax.dot_general(a, b, (((1,), (1,)), ((), ())), preferred_element_type=F32)
 
 
-def pack_kernel(depth, trig_ref, sino_ref, out_ref, rows_ref):
+def pack_kernel(depth, cos_ref, sin_ref, sino_ref, out_ref, rows_ref):
     views, z_count = sino_ref.shape[0], sino_ref.shape[1]
     rows = depth + 2 * HALO
     lane = iota((rows, LANES), 1)
@@ -62,8 +66,8 @@
         rows_ref[8 : 8 + z_count, :] = sino_ref[view, :, D0 : D0 + DW].astype(F32)
         rows_ref[8 + z_count : 16 + z_count, :] = zeros
         head = jnp.zeros((rows, LANES), F32)
-        for which in range(2):
-            left = jnp.full((rows, LANES), trig_ref[which, view], F32)
+        for which, trig_ref in enumerate((cos_ref, sin_ref)):
+            left = jnp.full((rows, LANES), trig_ref[view], F32)
             for part in range(3):
                 piece = left.astype(BF16).astype(F32)
                 left = left - piece
@@ -75,16 +79,17 @@
             out_ref[to, view, :, 0:LANES] = jnp.where(lane < 6, head, first).astype(BF16)
 
 
-def pack(trig, sino, group, depth):
+def pack(cosine, sine, sino, group, depth):
     views, z_count = sino.shape[0], sino.shape[1]
     return pl.pallas_call(
         functools.partial(pack_kernel, depth),
         out_shape=jax.ShapeDtypeStruct((group, views, depth + 2 * HALO, DW), BF16),
-        in_specs=[SMEM, VMEM],
+        in_specs=[SMEM, SMEM, VMEM],
         out_specs=VMEM,
         scratch_shapes=[pltpu.VMEM((z_count + 16, DW), F32)],
+        compiler_params=vmem_mib(6),
         name="pack",
-    )(trig, sino)
+    )(cosine, sine, sino)
 
 
 def project_kernel(scale, data_ref, ext_ref, own_ref, low_ref, high_ref, tab_ref, scal_ref, sem):
@@ -113,46 +118,76 @@
     high_ref[...] = pltpu.roll(values.reshape(views * rows, DW), DW - 1, 1).reshape(values.shape)
     copy.wait()
 
-    column = iota((Y, LANES), 1).astype(F32)
+    lane = iota((views, LANES), 1)
+    row_of_lane = (lane // (X // LANES) % Y).astype(F32) - edge
+    ends = jnp.floor(at(stop, row_of_lane)) - jnp.floor(at(start, row_of_lane))
+    apart = jnp.max(jnp.abs(ends)) >= float(LANES)
+
+    lanes = iota((Y, LANES), 1)
+    column = lanes.astype(F32)
     row_pos = iota((Y, LANES), 0).astype(F32) - edge
 
-    for block in range(X // LANES):
-        col = column + (block * LANES - (X - 1) / 2.0)
-
-        def one_view(view, sums):
-            tile = scal_ref[2, view, block].astype(jnp.int32)
-            position = col * scal_ref[0, view, 0] + row_pos * scal_ref[1, view, 0] + centre
-            lower = jnp.floor(position)
-            weight_low = jnp.maximum(0.0, 1.0 - jnp.abs(position - lower))
-            weight_high = jnp.maximum(0.0, 1.0 - jnp.abs(position - (lower + 1.0)))
-            weight_low = weight_low.astype(BF16).astype(F32)
-            weight_high = weight_high.astype(BF16).astype(F32)
-            index = lower.astype(jnp.int32) - (D0 + tile * LANES)
-            second = index >= LANES
-            index = jnp.bitwise_and(index, LANES - 1)
-            offset = pl.multiple_of(tile * LANES, LANES)
-
-            def take(ref, z):
-                def part(at_lane):
-                    line = jnp.broadcast_to(
-                        ref[view, z : z + 1, pl.ds(at_lane, LANES)], (Y, LANES)
-                    )
-                    return jnp.take_along_axis(line, index, axis=1, mode="promise_in_bounds")
-
-                return jnp.where(second, part(offset + LANES), part(offset))
-
-            return tuple(
-                sums[z] + (weight_low * take(low_ref, z) + weight_high * take(high_ref, z))
-                for z in range(rows)
-            )
-
-        empty = tuple(jnp.zeros((Y, LANES), F32) for _ in range(rows))
-        sums = lax.fori_loop(0, views, one_view, empty, unroll=8)
-        for z in range(rows):
-            done = sums[z] * scale
-            ext_ref[z, :, block * LANES : (block + 1) * LANES] = done
-            if HALO <= z < rows - HALO:
-                own_ref[z - HALO, :, block * LANES : (block + 1) * LANES] = done
+    def all_blocks(distinct):
+        def one_block(block, carry):
+            left = block.astype(F32) * LANES - (X - 1) / 2.0
+            col = column + left
+
+            def one_view(view, sums):
+                tile = scal_ref[2, view, block].astype(jnp.int32)
+                cos_part = scal_ref[0, view, 0]
+                sin_part = row_pos * scal_ref[1, view, 0]
+                position = col * cos_part + sin_part + centre
+                lower = jnp.floor(position)
+                weight_low = jnp.maximum(0.0, 1.0 - jnp.abs(position - lower))
+                weight_high = jnp.maximum(0.0, 1.0 - jnp.abs(position - (lower + 1.0)))
+                weight_low = weight_low.astype(BF16).astype(F32)
+                weight_high = weight_high.astype(BF16).astype(F32)
+                base = D0 + tile * LANES
+                index = lower.astype(jnp.int32) - base
+                second = index >= LANES
+                index = jnp.bitwise_and(index, LANES - 1)
+                offset = pl.multiple_of(tile * LANES, LANES)
+                if distinct:
+                    end1 = left * cos_part + sin_part + centre
+                    end2 = (left + (LANES - 1.0)) * cos_part + sin_part + centre
+                    least_index = jnp.floor(jnp.minimum(end1, end2)).astype(jnp.int32) - base
+                    in_first = lanes >= least_index
+
+                def take(ref, z):
+                    def line(at_lane):
+                        return jnp.broadcast_to(
+                            ref[view, z : z + 1, pl.ds(at_lane, LANES)], (Y, LANES)
+                        )
+
+                    def pick(values):
+                        return jnp.take_along_axis(
+                            values, index, axis=1, mode="promise_in_bounds"
+                        )
+
+                    one, two = line(offset), line(offset + LANES)
+                    if distinct:
+                        return pick(jnp.where(in_first, one, two))
+                    return jnp.where(second, pick(two), pick(one))
+
+                return tuple(
+                    sums[z] + (weight_low * take(low_ref, z) + weight_high * take(high_ref, z))
+                    for z in range(rows)
+                )
+
+            empty = tuple(jnp.zeros((Y, LANES), F32) for _ in range(rows))
+            sums = lax.fori_loop(0, views, one_view, empty, unroll=16 if distinct else 1)
+            cols = pl.ds(pl.multiple_of(block * LANES, LANES), LANES)
+            for z in range(rows):
+                done = sums[z] * scale
+                ext_ref[z, :, cols] = done
+                if HALO <= z < rows - HALO:
+                    own_ref[z - HALO, :, cols] = done
+            return carry
+
+        lax.fori_loop(0, X // LANES, one_block, 0)
+
+    pl.when(apart)(lambda: all_blocks(False))
+    pl.when(jnp.logical_not(apart))(lambda: all_blocks(True))
 
 
 def project(data, scale):
@@ -172,6 +207,7 @@
             pltpu.SMEM((3, views, LANES), F32),
             pltpu.SemaphoreType.DMA,
         ],
+        compiler_params=vmem_mib(14),
         name="project",
     )(data)
 
@@ -340,6 +376,7 @@
         cost_estimate=pl.CostEstimate(
             flops=20_000_000_000, bytes_accessed=2_000_000, transcendentals=0
         ),
+        compiler_params=vmem_mib(14),
         name="forward",
     )(ext, params)
 
@@ -406,11 +443,12 @@
 
     total = gather_taps(folded(acc1_ref), channels, first_column, True)
     total = total + gather_taps(folded(acc2_ref), channels, second_column, False)
-    lane = iota(total.shape, 1)
-    row = iota(total.shape, 0)
-    total = jnp.where((row == 0) & (lane == LOSS_AT), loss, total)
-    total = jnp.where((row == 0) & (lane == GRAD_B_SECOND_AT), grad_b2, total)
-    out_ref[...] = total
+    lane = iota((channels, LANES), 1)
+    diagonal = lane == iota((channels, LANES), 0)
+    line = jnp.sum(jnp.where(diagonal, total[:, TAPS : TAPS + 1], 0.0), axis=0, keepdims=True)
+    line = jnp.where(lane[0:8] == LOSS_AT, loss, jnp.broadcast_to(line, (8, LANES)))
+    out_ref[0:channels, :] = total
+    out_ref[channels : channels + 8, :] = jnp.where(lane[0:8] == GRAD_B_SECOND_AT, grad_b2, line)
 
 
 def backward(ext, pred, target, first, second, cells):
@@ -418,7 +456,7 @@
     height = first.shape[0]
     return pl.pallas_call(
         functools.partial(backward_kernel, cells),
-        out_shape=jax.ShapeDtypeStruct((height // Y, LANES), F32),
+        out_shape=jax.ShapeDtypeStruct((height // Y + 8, LANES), F32),
         in_specs=[VMEM] * 5,
         out_specs=VMEM,
         scratch_shapes=[
@@ -427,18 +465,40 @@
             pltpu.VMEM((2 * height, 2 * BLOCK), F32),
             pltpu.VMEM((2 * height, 2 * BLOCK), F32),
         ],
+        compiler_params=vmem_mib(20),
         name="backward",
     )(ext, pred, target, first, second)
 
 
-def sum_everywhere(value):
+def finish_kernel(one_ref, two_ref, loss_ref, w1_ref, b1_ref, w2_ref, b2_ref):
+    total = one_ref[...] + two_ref[...]
+    channels = w1_ref.shape[0]
+    line = total[channels : channels + 1]
+    loss_ref[...] = line[:, LOSS_AT : LOSS_AT + 1]
+    w1_ref[...] = total[0:channels, 0:TAPS]
+    b1_ref[...] = line[:, 0:channels]
+    w2_ref[...] = total[0:channels, W_SECOND_AT : W_SECOND_AT + TAPS]
+    b2_ref[...] = line[:, GRAD_B_SECOND_AT : GRAD_B_SECOND_AT + 1]
+
+
+def sum_everywhere(value, channels):
     devices = lax.axis_size("subset") * lax.axis_size("slab")
     apart = 1
-    while apart < devices:
-        pairs = [(i, i ^ apart) for i in range(devices)]
-        value = value + lax.ppermute(value, BOTH, pairs)
+    while True:
+        arrived = lax.ppermute(value, BOTH, [(i, i ^ apart) for i in range(devices)])
         apart *= 2
-    return value
+        if apart == devices:
+            break
+        value = value + arrived
+    shapes = ((1, 1), (channels, TAPS), (1, channels), (channels, TAPS), (1, 1))
+    return pl.pallas_call(
+        finish_kernel,
+        out_shape=tuple(jax.ShapeDtypeStruct(shape, F32) for shape in shapes),
+        in_specs=[VMEM, VMEM],
+        out_specs=(VMEM,) * 5,
+        compiler_params=vmem_mib(1),
+        name="finish",
+    )(value, arrived)
 
 
 def body(sinogram, angles, w_first, b_first, w_second, b_second):
@@ -453,7 +513,6 @@
     cells = float(n_sub * z_count * Y * X)
     assert devices & (devices - 1) == 0 and channels == 32 and depth >= HALO
 
-    trig = jnp.stack([jnp.cos(angles), jnp.sin(angles)])
     params = jnp.concatenate(
         [
             w_first,
@@ -464,7 +523,7 @@
         ],
         axis=1,
     )
-    sent = pack(trig, sinogram, group, depth)
+    sent = pack(jnp.cos(angles), jnp.sin(angles), sinogram, group, depth)
     groups = [list(range(s * group, (s + 1) * group)) for s in range(n_sub)]
     got = lax.all_to_all(sent, BOTH, 0, 0, axis_index_groups=groups)
     got = got.reshape(group * local_views, depth + 2 * HALO, DW)
@@ -479,15 +538,15 @@
 
     pred, first, second = forward(ext, params)
     partial = backward(ext, pred, target, first, second, cells)
-    total = sum_everywhere(partial)
+    loss, grad_w1, grad_b1, grad_w2, grad_b2 = sum_everywhere(partial, channels)
     return (
         pred[None],
         target[None],
-        total[0, LOSS_AT],
-        total[:, 0:TAPS],
-        total[:, TAPS],
-        total[:, W_SECOND_AT : W_SECOND_AT + TAPS],
-        total[0, GRAD_B_SECOND_AT : GRAD_B_SECOND_AT + 1],
+        loss.reshape(()),
+        grad_w1,
+        grad_b1.reshape(-1),
+        grad_w2,
+        grad_b2.reshape(-1),
     )
 
 

time: 86.9 us -> 74.6 us (0.86)
  Pallas kernels: 34.8 us -> 25.2 us
  local copies, waits for them, and re-layouts: 6.97 us -> 4.84 us
  other arithmetic: 1.31 us -> 0.02 us
    pallas_call x1, Pallas kernels: 15.5 us -> 8.38 us  [project(): pl.pallas_call(functools.partial(project_kernel, scale), out_shape=(jax.S...]
    slice x3 -> x0, local copies, waits for them, and re-layouts: 1.96 us -> none  [the longest x1 0.69 us: body(): total[:, TAPS]]
    pallas_call x1, Pallas kernels: 10.6 us -> 8.92 us  [backward(): pl.pallas_call(functools.partial(backward_kernel, cells), out_shape=jax.S...]
    pallas_call x1, Pallas kernels: 6.57 us -> 5.62 us  [forward(): pl.pallas_call(forward_kernel, out_shape=(jax.ShapeDtypeStruct((rows - 2...]
    unnamed x13 -> x11, local copies, waits for them, and re-layouts: 3.53 us -> 3.97 us
  transfers between devices with their start and end apart: 7 -> 7, of which waited for: 6 -> 6; matrix products, arithmetic and copies ran while one was open for 1% -> 0% of each run, Pallas kernels for 8% -> 8%
where the time goes in v1:
time: 74.6 us; the launch traced here: 74.2 us
  waiting for transfers between devices  31.6 us (42%)
  Pallas kernels  25.2 us (34%)
  starting transfers between devices  11.1 us (15%)
  local copies, waits for them, and re-layouts  4.84 us (6%)
  between operations  1.34 us (2%)
    all_to_all x1, waiting for transfers between devices, body(): got = lax.all_to_all(sent, BOTH, 0, 0, axis_index_groups=groups)  16.3 us
    ppermute x5, waiting for transfers between devices, sum_everywhere(): lax.ppermute(value, BOTH, [(i, i ^ apart) for i in range(devices)])  15.3 us
    pallas_call x1, Pallas kernels, backward(): pl.pallas_call(functools.partial(backward_kernel, cells), out_shape=jax.S...  8.92 us
    pallas_call x1, Pallas kernels, project(): pl.pallas_call(functools.partial(project_kernel, scale), out_shape=(jax.S...  8.38 us
    all_to_all x1, starting transfers between devices, body(): got = lax.all_to_all(sent, BOTH, 0, 0, axis_index_groups=groups)  7.41 us
    pallas_call x1, Pallas kernels, forward(): pl.pallas_call(forward_kernel, out_shape=(jax.ShapeDtypeStruct((rows - 2...  5.62 us
    unnamed x11, local copies, waits for them, and re-layouts  3.97 us
    ppermute x5, starting transfers between devices, sum_everywhere(): lax.ppermute(value, BOTH, [(i, i ^ apart) for i in range(devices)])  2.16 us
  transfers between devices with their start and end apart: 7, of which 6 were waited for; matrix products, arithmetic and copies ran while one was open for 0% of the time, Pallas kernels for 8%

profile of v1, /device:TPU:0, one launch (start us, length us, event | category | flops | bytes accessed | tf_op | source)
XLA Modules:
  0.0 74.2 jit_solution(16741286932669755646)
XLA Ops:
  0.6 0.7 fusion
  1.3 0.0 copy-start
  1.3 1.0 %copy-done = bf16[2,64,2048]{2,1,0:T(8,128)(2,1)S(1)} copy-done((bf16[2,64,2048]{2,1,0:T(8,128)(2,1)S(1)}, bf16[2,64,2048]{2,1,0:T(8,128)(2,1)}, u32[]{:S(2)}) %copy-start) | copy-done | bytes 524312
  2.4 1.6 %pack.1 = bf16[16,2,8,1280]{3,2,1,0:T(8,128)(2,1)} custom-call(f32[2]{0:T(128)S(1)} %get-tuple-element.28.cos_ref, f32[2]{0:T(128)S(1)} %get-tuple-element.27.sin_ref, bf16[2,64,2048]{2,1,0:T(8,128)(2,1)S(1)} %copy-done), custom_call_target="tpu_custom_call" | custom-call | tf_op jit(solution)/shard_map/pack/pallas_call | solution.py:84
  4.0 7.4 %all-to-all-start = ((bf16[16,2,8,1280]{3,2,1,0:T(8,128)(2,1)}), bf16[16,2,8,1280]{3,2,1,0:T(8,128)(2,1)S(1)}, u32[]{:S(2)}, u32[]{:S(2)}) async-start(bf16[16,2,8,1280]{3,2,1,0:T(8,128)(2,1)} %pack.1), calls=%async_computation | async-start | bytes 1310720 | tf_op jit(solution)/shard_map/all_to_all | solution.py:528
  12.1 0.0 copy-start.4
  12.1 0.6 copy-done.4
  12.7 0.1 copy.13
  12.8 0.0 copy-start.2
  12.8 0.0 copy-start.3
  12.8 0.7 copy-done.2
  13.5 0.0 copy-done.3
  13.6 0.1 concatenate.3.params_ref
  13.6 16.3 %all-to-all-done = bf16[16,2,8,1280]{3,2,1,0:T(8,128)(2,1)S(1)} async-done(((bf16[16,2,8,1280]{3,2,1,0:T(8,128)(2,1)}), bf16[16,2,8,1280]{3,2,1,0:T(8,128)(2,1)S(1)}, u32[]{:S(2)}, u32[]{:S(2)}) %all-to-all-start) | async-done | bytes 655392 | tf_op jit(solution)/shard_map/all_to_all | solution.py:528
  29.9 8.4 %project.1 = (f32[8,8,1024]{2,1,0:T(8,128)S(1)}, f32[4,8,1024]{2,1,0:T(8,128)S(1)}) custom-call(bf16[32,8,1280]{2,1,0:T(8,128)(2,1)S(1)} %bitcast.9), custom_call_target="tpu_custom_call" | custom-call | tf_op jit(solution)/shard_map/project/pallas_call | solution.py:195
  38.3 1.6 %collective-permute-start = (f32[4,8,1024]{2,1,0:T(8,128)S(1)}, f32[4,8,1024]{2,1,0:T(8,128)S(1)}, u32[]{:S(2)}, u32[]{:S(2)}) collective-permute-start(f32[4,8,1024]{2,1,0:T(8,128)S(1)} %get-tuple-element.19), channel_id=1, source_target_pairs={{0,16},{1,17},{2,18},{3,19},{4,20},{5,21},{6,22},{7,23},{8,24},{9,... | collective-permute-start | bytes 393224 | tf_op jit(solution)/shard_map/ppermute | solution.py:535
  39.9 5.6 %forward.1 = (f32[4,8,1024]{2,1,0:T(8,128)}, bf16[256,256]{1,0:T(8,128)(2,1)S(1)}, bf16[256,256]{1,0:T(8,128)(2,1)S(1)}) custom-call(f32[8,8,1024]{2,1,0:T(8,128)S(1)} %get-tuple-element.17.ext_ref, f32[32,128]{1,0:T(8,128)S(1)} %concatenate.3.params_ref), custom_call_target="tpu_custom_call" | custom-call | flops 20000000000 | bytes 2000000 | tf_op jit(solution)/shard_map/forward/pallas_call | solution.py:363
  45.5 0.0 collective-permute-done.target_ref
  45.5 0.0 copy-start.1
  45.5 0.9 %copy-done.1 = f32[4,8,1024]{2,1,0:T(8,128)S(1)} copy-done((f32[4,8,1024]{2,1,0:T(8,128)S(1)}, f32[4,8,1024]{2,1,0:T(8,128)}, u32[]{:S(2)}) %copy-start.1) | copy-done | bytes 131096
  46.4 8.9 %backward.1 = f32[40,128]{1,0:T(8,128)S(1)} custom-call(f32[8,8,1024]{2,1,0:T(8,128)S(1)} %get-tuple-element.17.ext_ref, f32[4,8,1024]{2,1,0:T(8,128)S(1)} %copy-done.1, f32[4,8,1024]{2,1,0:T(8,128)S(1)} %collective-permute-done.target_ref, bf16[256,256]{1,0:T(8,128)(2,1)S(1)} %get-tuple-element.20.first_ref, bf16[256,256]{1,0:T(8,128)(2,1)S(1)} %get-tuple-element.21.second_ref), custom_call_target="tpu_custom_call" | custom-call | tf_op jit(solution)/shard_map/backward/pallas_call | solution.py:457
  55.3 0.6 collective-permute-start.1
  55.9 3.2 %collective-permute-done.1 = f32[40,128]{1,0:T(8,128)S(1)} collective-permute-done((f32[40,128]{1,0:T(8,128)S(1)}, f32[40,128]{1,0:T(8,128)S(1)}, u32[]{:S(2)}, u32[]{:S(2)}) %collective-permute-start.1) | collective-permute-done | bytes 20512 | tf_op jit(solution)/shard_map/ppermute | solution.py:488
  59.2 1.0 %collective-permute-start.2 = (f32[40,128]{1,0:T(8,128)S(1)}, f32[40,128]{1,0:T(8,128)S(1)}, u32[]{:S(2)}, u32[]{:S(2)}) collective-permute-start(f32[40,128]{1,0:T(8,128)S(1)} %add.12), channel_id=1, source_target_pairs={{0,2},{1,3},{2,0},{3,1},{4,6},{5,7},{6,4},{7,5},{8,10},{9,11},{10,... | collective-permute-start | bytes 61448 | tf_op jit(solution)/shard_map/ppermute | solution.py:488
  60.2 3.0 %collective-permute-done.2 = f32[40,128]{1,0:T(8,128)S(1)} collective-permute-done((f32[40,128]{1,0:T(8,128)S(1)}, f32[40,128]{1,0:T(8,128)S(1)}, u32[]{:S(2)}, u32[]{:S(2)}) %collective-permute-start.2) | collective-permute-done | bytes 20512 | tf_op jit(solution)/shard_map/ppermute | solution.py:488
  63.2 0.0 collective-permute-start.3
  63.2 4.7 %collective-permute-done.3 = f32[40,128]{1,0:T(8,128)S(1)} collective-permute-done((f32[40,128]{1,0:T(8,128)S(1)}, f32[40,128]{1,0:T(8,128)S(1)}, u32[]{:S(2)}, u32[]{:S(2)}) %collective-permute-start.3) | collective-permute-done | bytes 20512 | tf_op jit(solution)/shard_map/ppermute | solution.py:488
  67.9 0.0 collective-permute-start.4
  67.9 1.2 %collective-permute-done.4 = f32[40,128]{1,0:T(8,128)S(1)} collective-permute-done((f32[40,128]{1,0:T(8,128)S(1)}, f32[40,128]{1,0:T(8,128)S(1)}, u32[]{:S(2)}, u32[]{:S(2)}) %collective-permute-start.4) | collective-permute-done | bytes 20512 | tf_op jit(solution)/shard_map/ppermute | solution.py:488
  69.1 0.5 collective-permute-start.5
  69.6 3.2 %collective-permute-done.5.two_ref = f32[40,128]{1,0:T(8,128)S(1)} collective-permute-done((f32[40,128]{1,0:T(8,128)S(1)}, f32[40,128]{1,0:T(8,128)S(1)}, u32[]{:S(2)}, u32[]{:S(2)}) %collective-permute-start.5) | collective-permute-done | bytes 20512 | tf_op jit(solution)/shard_map/ppermute | solution.py:488
  72.8 0.7 finish.1
  73.5 0.7 copy.16
  (6 shorter events, 0.0 us)
Async XLA Ops:
  1.3 1.0 %copy-start = (bf16[2,64,2048]{2,1,0:T(8,128)(2,1)S(1)}, bf16[2,64,2048]{2,1,0:T(8,128)(2,1)}, u32[]{:S(2)}) copy-start(bf16[2,64,2048]{2,1,0:T(8,128)(2,1)} %sino_ref.1) | copy-start | bytes 1572868
  4.0 25.9 %all-to-all-start = ((bf16[16,2,8,1280]{3,2,1,0:T(8,128)(2,1)}), bf16[16,2,8,1280]{3,2,1,0:T(8,128)(2,1)S(1)}, u32[]{:S(2)}, u32[]{:S(2)}) async-start(bf16[16,2,8,1280]{3,2,1,0:T(8,128)(2,1)} %pack.1), calls=%async_computation | async-start | bytes 1310720 | tf_op jit(solution)/shard_map/all_to_all | solution.py:528
  12.1 0.7 copy-start.4
  12.8 0.7 copy-start.2
  12.8 0.7 copy-start.3
  38.3 7.2 %collective-permute-start = (f32[4,8,1024]{2,1,0:T(8,128)S(1)}, f32[4,8,1024]{2,1,0:T(8,128)S(1)}, u32[]{:S(2)}, u32[]{:S(2)}) collective-permute-start(f32[4,8,1024]{2,1,0:T(8,128)S(1)} %get-tuple-element.19), channel_id=1, source_target_pairs={{0,16},{1,17},{2,18},{3,19},{4,20},{5,21},{6,22},{7,23},{8,24},{9,... | collective-permute-start | bytes 393224 | tf_op jit(solution)/shard_map/ppermute | solution.py:535
  45.5 0.9 %copy-start.1 = (f32[4,8,1024]{2,1,0:T(8,128)S(1)}, f32[4,8,1024]{2,1,0:T(8,128)}, u32[]{:S(2)}) copy-start(f32[4,8,1024]{2,1,0:T(8,128)} %get-tuple-element.18.pred_ref) | copy-start | bytes 393220
  55.3 3.8 %collective-permute-start.1 = (f32[40,128]{1,0:T(8,128)S(1)}, f32[40,128]{1,0:T(8,128)S(1)}, u32[]{:S(2)}, u32[]{:S(2)}) collective-permute-start(f32[40,128]{1,0:T(8,128)S(1)} %backward.1), channel_id=1, source_target_pairs={{0,1},{1,0},{2,3},{3,2},{4,5},{5,4},{6,7},{7,6},{8,9},{9,8},{10,11... | collective-permute-start | bytes 61448 | tf_op jit(solution)/shard_map/ppermute | solution.py:488
  59.2 4.0 %collective-permute-start.2 = (f32[40,128]{1,0:T(8,128)S(1)}, f32[40,128]{1,0:T(8,128)S(1)}, u32[]{:S(2)}, u32[]{:S(2)}) collective-permute-start(f32[40,128]{1,0:T(8,128)S(1)} %add.12), channel_id=1, source_target_pairs={{0,2},{1,3},{2,0},{3,1},{4,6},{5,7},{6,4},{7,5},{8,10},{9,11},{10,... | collective-permute-start | bytes 61448 | tf_op jit(solution)/shard_map/ppermute | solution.py:488
  63.2 4.7 %collective-permute-start.3 = (f32[40,128]{1,0:T(8,128)S(1)}, f32[40,128]{1,0:T(8,128)S(1)}, u32[]{:S(2)}, u32[]{:S(2)}) collective-permute-start(f32[40,128]{1,0:T(8,128)S(1)} %add.13), channel_id=1, source_target_pairs={{0,4},{1,5},{2,6},{3,7},{4,0},{5,1},{6,2},{7,3},{8,12},{9,13},{10,... | collective-permute-start | bytes 61448 | tf_op jit(solution)/shard_map/ppermute | solution.py:488
  67.9 1.2 %collective-permute-start.4 = (f32[40,128]{1,0:T(8,128)S(1)}, f32[40,128]{1,0:T(8,128)S(1)}, u32[]{:S(2)}, u32[]{:S(2)}) collective-permute-start(f32[40,128]{1,0:T(8,128)S(1)} %add.14), channel_id=1, source_target_pairs={{0,8},{1,9},{2,10},{3,11},{4,12},{5,13},{6,14},{7,15},{8,0},{9,1},... | collective-permute-start | bytes 61448 | tf_op jit(solution)/shard_map/ppermute | solution.py:488
  69.1 3.8 %collective-permute-start.5 = (f32[40,128]{1,0:T(8,128)S(1)}, f32[40,128]{1,0:T(8,128)S(1)}, u32[]{:S(2)}, u32[]{:S(2)}) collective-permute-start(f32[40,128]{1,0:T(8,128)S(1)} %add.15.one_ref), channel_id=1, source_target_pairs={{0,16},{1,17},{2,18},{3,19},{4,20},{5,21},{6,22},{7,23},{8,24},{9,... | collective-permute-start | bytes 61448 | tf_op jit(solution)/shard_map/ppermute | solution.py:488

commit v2 on v1

--- a/solution.py
+++ b/solution.py
@@ -56,22 +56,31 @@
     return lax.dot_general(a, b, (((1,), (1,)), ((), ())), preferred_element_type=F32)
 
 
-def pack_kernel(depth, cos_ref, sin_ref, sino_ref, out_ref, rows_ref):
+def pack_kernel(depth, angle_ref, sino_ref, out_ref, held_ref, rows_ref, sems):
     views, z_count = sino_ref.shape[0], sino_ref.shape[1]
     rows = depth + 2 * HALO
+    copies = [
+        pltpu.make_async_copy(
+            sino_ref.at[view, :, pl.ds(D0, DW)], held_ref.at[view], sems.at[view]
+        )
+        for view in range(views)
+    ]
+    for copy in copies:
+        copy.start()
     lane = iota((rows, LANES), 1)
     zeros = jnp.zeros((8, DW), F32)
+    rows_ref[0:8, :] = zeros
+    rows_ref[8 + z_count : 16 + z_count, :] = zeros
     for view in range(views):
-        rows_ref[0:8, :] = zeros
-        rows_ref[8 : 8 + z_count, :] = sino_ref[view, :, D0 : D0 + DW].astype(F32)
-        rows_ref[8 + z_count : 16 + z_count, :] = zeros
+        angle = jnp.full((rows, LANES), angle_ref[view], F32)
         head = jnp.zeros((rows, LANES), F32)
-        for which, trig_ref in enumerate((cos_ref, sin_ref)):
-            left = jnp.full((rows, LANES), trig_ref[view], F32)
+        for which, left in enumerate((jnp.cos(angle), jnp.sin(angle))):
             for part in range(3):
                 piece = left.astype(BF16).astype(F32)
                 left = left - piece
                 head = jnp.where(lane == 3 * which + part, piece, head)
+        copies[view].wait()
+        rows_ref[8 : 8 + z_count, :] = held_ref[view].astype(F32)
         for to in range(out_ref.shape[0]):
             start = 8 + to * depth - HALO
             out_ref[to, view] = rows_ref[start : start + rows, :].astype(BF16)
@@ -79,17 +88,20 @@
             out_ref[to, view, :, 0:LANES] = jnp.where(lane < 6, head, first).astype(BF16)
 
 
-def pack(cosine, sine, sino, group, depth):
+def pack(angles, sino, group, depth):
     views, z_count = sino.shape[0], sino.shape[1]
     return pl.pallas_call(
         functools.partial(pack_kernel, depth),
         out_shape=jax.ShapeDtypeStruct((group, views, depth + 2 * HALO, DW), BF16),
-        in_specs=[SMEM, SMEM, VMEM],
+        in_specs=[SMEM, pl.BlockSpec(memory_space=pltpu.HBM)],
         out_specs=VMEM,
-        scratch_shapes=[pltpu.VMEM((z_count + 16, DW), F32)],
-        compiler_params=vmem_mib(6),
+        scratch_shapes=[
+            pltpu.VMEM((views, z_count, DW), BF16),
+            pltpu.VMEM((z_count + 16, DW), F32),
+            pltpu.SemaphoreType.DMA((views,)),
+        ],
         name="pack",
-    )(cosine, sine, sino)
+    )(angles, sino)
 
 
 def project_kernel(scale, data_ref, ext_ref, own_ref, low_ref, high_ref, tab_ref, scal_ref, sem):
@@ -114,8 +126,11 @@
     copy = pltpu.make_async_copy(tab_ref, scal_ref, sem)
     copy.start()
     values = data_ref[...].astype(F32)
-    low_ref[...] = values
-    high_ref[...] = pltpu.roll(values.reshape(views * rows, DW), DW - 1, 1).reshape(values.shape)
+    moved = pltpu.roll(values.reshape(views * rows, DW), DW - 1, 1).reshape(values.shape)
+    for tile in range(DW // LANES):
+        cols = slice(tile * LANES, (tile + 1) * LANES)
+        low_ref[:, tile] = values[:, :, cols]
+        high_ref[:, tile] = moved[:, :, cols]
     copy.wait()
 
     lane = iota((views, LANES), 1)
@@ -146,7 +161,6 @@
                 index = lower.astype(jnp.int32) - base
                 second = index >= LANES
                 index = jnp.bitwise_and(index, LANES - 1)
-                offset = pl.multiple_of(tile * LANES, LANES)
                 if distinct:
                     end1 = left * cos_part + sin_part + centre
                     end2 = (left + (LANES - 1.0)) * cos_part + sin_part + centre
@@ -154,17 +168,15 @@
                     in_first = lanes >= least_index
 
                 def take(ref, z):
-                    def line(at_lane):
-                        return jnp.broadcast_to(
-                            ref[view, z : z + 1, pl.ds(at_lane, LANES)], (Y, LANES)
-                        )
+                    def line(at_tile):
+                        return ref[view, at_tile, pl.ds(z, Y, stride=0), :]
 
                     def pick(values):
                         return jnp.take_along_axis(
                             values, index, axis=1, mode="promise_in_bounds"
                         )
 
-                    one, two = line(offset), line(offset + LANES)
+                    one, two = line(tile), line(tile + 1)
                     if distinct:
                         return pick(jnp.where(in_first, one, two))
                     return jnp.where(second, pick(two), pick(one))
@@ -201,8 +213,8 @@
         in_specs=[VMEM],
         out_specs=(VMEM, VMEM),
         scratch_shapes=[
-            pltpu.VMEM((views, rows, DW), F32),
-            pltpu.VMEM((views, rows, DW), F32),
+            pltpu.VMEM((views, DW // LANES, rows, LANES), F32),
+            pltpu.VMEM((views, DW // LANES, rows, LANES), F32),
             pltpu.VMEM((3, views, LANES), F32),
             pltpu.SMEM((3, views, LANES), F32),
             pltpu.SemaphoreType.DMA,
@@ -257,33 +269,30 @@
     return total.astype(BF16)
 
 
-def gather_taps(grad, channels, column_of, bias):
+def gather_taps(grads, channels):
     height = channels * Y
-    rep = (iota((channels, height), 1) // Y == iota((channels, height), 0)).astype(F32)
-    col = iota((height, BLOCK), 1)
-    row_y = iota((height, BLOCK), 0) % Y
-    inner = iota((BLOCK, LANES), 0)
-    to = iota((BLOCK, LANES), 1)
-    total = jnp.zeros((channels, LANES), F32)
-    for dy in range(3):
-        here = (col < 72) & (col % 8 - row_y + 1 == dy)
-        pick = (inner < 72) & (to == column_of(inner // 24, (inner // 8) % 3, dy))
-        if bias and dy == 1:
-            here = here | (col == 72)
-            pick = pick | ((inner == 72) & (to == TAPS))
-        summed = jnp.dot(
-            rep,
-            jnp.where(here, grad, 0.0),
-            precision=lax.Precision.HIGHEST,
-            preferred_element_type=F32,
-        )
-        total = total + jnp.dot(
-            summed,
-            pick.astype(F32),
-            precision=lax.Precision.HIGHEST,
-            preferred_element_type=F32,
-        )
-    return total
+    col = iota((height, LANES), 1)
+    row_y = iota((height, LANES), 0) % Y
+    inner = iota((LANES, LANES), 0)
+    to = iota((LANES, LANES), 1)
+    pieces = []
+    picks = []
+    for grad, column_of, bias in grads:
+        for dy in range(3):
+            here = (col < 72) & (col % 8 - row_y + 1 == dy)
+            pick = (inner < 72) & (to == column_of(inner // 24, (inner // 8) % 3, dy))
+            if bias and dy == 1:
+                here = here | (col == 72)
+                pick = pick | ((inner == 72) & (to == TAPS))
+            masked = jnp.where(here, grad, 0.0).reshape(channels, Y, LANES)
+            pieces.append(jnp.sum(masked, axis=1))
+            picks.append(pick.astype(F32))
+    return jnp.dot(
+        jnp.concatenate(pieces, axis=1),
+        jnp.concatenate(picks, axis=0),
+        precision=lax.Precision.HIGHEST,
+        preferred_element_type=F32,
+    )
 
 
 def shift_columns(value, by):
@@ -321,28 +330,52 @@
     return jnp.where(outside, 0.0, 1.0).astype(F32)
 
 
-def forward_kernel(ext_ref, params_ref, pred_ref, first_ref, second_ref, shifted_ref, acc_ref):
+def weights_kernel(params_ref, first_ref, second_ref, turned_ref):
+    params = params_ref[...]
+    second = spread(params, second_column, False)
+    first_ref[...] = spread(params, first_column, True)
+    second_ref[...] = second
+    turned_ref[...] = second.astype(F32).T.astype(BF16)
+
+
+def weights(params):
+    height = params.shape[0] * Y
+    return pl.pallas_call(
+        weights_kernel,
+        out_shape=(
+            jax.ShapeDtypeStruct((height, TILE), BF16),
+            jax.ShapeDtypeStruct((height, TILE), BF16),
+            jax.ShapeDtypeStruct((TILE, height), BF16),
+        ),
+        in_specs=[VMEM],
+        out_specs=(VMEM,) * 3,
+        compiler_params=vmem_mib(8),
+        name="weights",
+    )(params)
+
+
+def forward_kernel(
+    ext_ref, params_ref, first_ref, turned_ref, pred_ref, again_ref, shifted_ref, hidden_ref, acc_ref
+):
     rows = ext_ref.shape[0]
     hidden_count = rows - 2
-    params = params_ref[...]
-    first = spread(params, first_column, True)
-    second = spread(params, second_column, False)
-    first_ref[...] = first
-    second_ref[...] = second
-    second_t = second.astype(F32).T.astype(BF16)
+    height = first_ref.shape[0]
+    first = first_ref[...]
     fill_shifted(shifted_ref, ext_ref[...].reshape(rows * Y, X))
     acc_ref[...] = jnp.zeros(acc_ref.shape, F32)
 
     def one_slice(hidden_slice, carry):
         flag = slice_flag(hidden_slice, hidden_count)
         at = pl.multiple_of(hidden_slice * Y, Y)
+        kept = pl.ds(pl.multiple_of(hidden_slice * height, height), height)
         for tile in range(X // TILE):
             cols = slice(tile * TILE, (tile + 1) * TILE)
             high, low = patch(shifted_ref, hidden_slice, tile)
             hidden = jnp.maximum(apply_spread(first, high, low), 0.0) * flag
             h_high, h_low = split2(hidden)
-            main = dot(second_t[BLOCK : 3 * BLOCK], h_high)
-            taps = main[0:BLOCK] + main[BLOCK : 2 * BLOCK] + dot(second_t[0:BLOCK], h_low)
+            hidden_ref[kept, cols] = h_high
+            main = dot(turned_ref[BLOCK : 3 * BLOCK], h_high)
+            taps = main[0:BLOCK] + main[BLOCK : 2 * BLOCK] + dot(turned_ref[0:BLOCK], h_low)
             for dx in range(3):
                 acc_ref[dx, pl.ds(at, 3 * Y), cols] += taps[24 * dx : 24 * dx + 24]
         return carry
@@ -353,56 +386,63 @@
     for dx in (0, 2):
         added = added + shift_columns(acc_ref[dx, inner, :], 1 - dx)
     own = ext_ref[HALO : rows - HALO].reshape(added.shape)
-    bias = params[0:1, B_SECOND_AT : B_SECOND_AT + 1]
-    pred_ref[...] = (own + added + bias).reshape(pred_ref.shape)
-
-
-def forward(ext, params):
+    bias = params_ref[0:1, B_SECOND_AT : B_SECOND_AT + 1]
+    pred = (own + added + bias).reshape(pred_ref.shape)
+    pred_ref[...] = pred
+    again_ref[...] = pred
+
+
+def forward(ext, params, first, turned):
     rows = ext.shape[0]
-    height = params.shape[0] * Y
+    height = first.shape[0]
+    own = jax.ShapeDtypeStruct((rows - 2 * HALO, Y, X), F32)
     return pl.pallas_call(
         forward_kernel,
         out_shape=(
-            jax.ShapeDtypeStruct((rows - 2 * HALO, Y, X), F32),
-            jax.ShapeDtypeStruct((height, TILE), BF16),
-            jax.ShapeDtypeStruct((height, TILE), BF16),
+            own,
+            own,
+            jax.ShapeDtypeStruct((3, rows * Y, X), F32),
+            jax.ShapeDtypeStruct(((rows - 2) * height, X), BF16),
         ),
-        in_specs=[VMEM, VMEM],
-        out_specs=(VMEM, VMEM, VMEM),
-        scratch_shapes=[
-            pltpu.VMEM((3, rows * Y, X), F32),
-            pltpu.VMEM((3, rows * Y, X), F32),
-        ],
+        in_specs=[VMEM] * 4,
+        out_specs=(VMEM,) * 4,
+        scratch_shapes=[pltpu.VMEM((3, rows * Y, X), F32)],
         cost_estimate=pl.CostEstimate(
             flops=20_000_000_000, bytes_accessed=2_000_000, transcendentals=0
         ),
-        compiler_params=vmem_mib(14),
+        compiler_params=vmem_mib(18),
         name="forward",
-    )(ext, params)
+    )(ext, params, first, turned)
+
+
+def padded_rows(high, low):
+    none = jnp.zeros((LANES - BLOCK, high.shape[1]), BF16)
+    return jnp.concatenate([high, none, low, none], axis=0)
 
 
 def backward_kernel(
     cells,
-    ext_ref,
+    shifted_ref,
+    hidden_ref,
     pred_ref,
     target_ref,
-    first_ref,
     second_ref,
     out_ref,
-    shifted_ref,
+    target_out_ref,
     grad_ref,
     acc1_ref,
     acc2_ref,
 ):
-    rows = ext_ref.shape[0]
+    rows = shifted_ref.shape[1] // Y
     hidden_count = rows - 2
-    height = first_ref.shape[0]
+    height = second_ref.shape[0]
     channels = height // Y
-    diff = (pred_ref[...] - target_ref[...]).reshape((rows - 2 * HALO) * Y, X)
+    target = target_ref[...]
+    target_out_ref[...] = target
+    diff = (pred_ref[...] - target).reshape((rows - 2 * HALO) * Y, X)
     resid = 2.0 * diff / cells
     loss = jnp.sum(diff * diff, keepdims=True) / cells
     grad_b2 = jnp.sum(resid, keepdims=True)
-    fill_shifted(shifted_ref, ext_ref[...].reshape(rows * Y, X))
     inner = slice(HALO * Y, (rows - HALO) * Y)
     for dx in range(3):
         grad_ref[dx, 0 : HALO * Y, :] = jnp.zeros((HALO * Y, X), F32)
@@ -410,24 +450,21 @@
         grad_ref[dx, inner, :] = shift_columns(resid, dx - 1)
     acc1_ref[...] = jnp.zeros(acc1_ref.shape, F32)
     acc2_ref[...] = jnp.zeros(acc2_ref.shape, F32)
-    first = first_ref[...]
     second = second_ref[...]
 
     def one_slice(hidden_slice, carry):
-        flag = slice_flag(hidden_slice, hidden_count)
+        kept = pl.ds(pl.multiple_of(hidden_slice * height, height), height)
         sum1 = None
         sum2 = None
         for tile in range(X // TILE):
+            cols = slice(tile * TILE, (tile + 1) * TILE)
             high, low = patch(shifted_ref, hidden_slice, tile)
             g_high, g_low = patch(grad_ref, hidden_slice, tile)
-            hidden = jnp.maximum(apply_spread(first, high, low), 0.0) * flag
-            grad_pre = jnp.where(hidden > 0.0, apply_spread(second, g_high, g_low), 0.0)
-            part1 = dot_nt(
-                jnp.concatenate(split2(grad_pre), axis=0), jnp.concatenate([high, low], axis=0)
-            )
-            part2 = dot_nt(
-                jnp.concatenate(split2(hidden), axis=0), jnp.concatenate([g_high, g_low], axis=0)
-            )
+            hidden = hidden_ref[kept, cols]
+            grad_hidden = apply_spread(second, g_high, g_low)
+            grad_pre = jnp.where(hidden.astype(F32) > 0.0, grad_hidden, 0.0).astype(BF16)
+            part1 = dot_nt(grad_pre, padded_rows(high, low))
+            part2 = dot_nt(hidden, padded_rows(g_high, g_low))
             sum1 = part1 if sum1 is None else sum1 + part1
             sum2 = part2 if sum2 is None else sum2 + part2
         acc1_ref[...] += sum1
@@ -437,12 +474,11 @@
     lax.fori_loop(0, hidden_count, one_slice, 0)
 
     def folded(ref):
-        value = ref[...]
-        value = value[0:height] + value[height : 2 * height]
-        return value[:, 0:BLOCK] + value[:, BLOCK : 2 * BLOCK]
-
-    total = gather_taps(folded(acc1_ref), channels, first_column, True)
-    total = total + gather_taps(folded(acc2_ref), channels, second_column, False)
+        return ref[:, 0:LANES] + ref[:, LANES : 2 * LANES]
+
+    total = gather_taps(
+        ((folded(acc1_ref), first_column, True), (folded(acc2_ref), second_column, False)), channels
+    )
     lane = iota((channels, LANES), 1)
     diagonal = lane == iota((channels, LANES), 0)
     line = jnp.sum(jnp.where(diagonal, total[:, TAPS : TAPS + 1], 0.0), axis=0, keepdims=True)
@@ -451,23 +487,24 @@
     out_ref[channels : channels + 8, :] = jnp.where(lane[0:8] == GRAD_B_SECOND_AT, grad_b2, line)
 
 
-def backward(ext, pred, target, first, second, cells):
-    rows = ext.shape[0]
-    height = first.shape[0]
+def backward(shifted, hidden, pred, target, second, cells):
+    height = second.shape[0]
     return pl.pallas_call(
         functools.partial(backward_kernel, cells),
-        out_shape=jax.ShapeDtypeStruct((height // Y + 8, LANES), F32),
+        out_shape=(
+            jax.ShapeDtypeStruct((height // Y + 8, LANES), F32),
+            jax.ShapeDtypeStruct(target.shape, F32),
+        ),
         in_specs=[VMEM] * 5,
-        out_specs=VMEM,
+        out_specs=(VMEM, VMEM),
         scratch_shapes=[
-            pltpu.VMEM((3, rows * Y, X), F32),
-            pltpu.VMEM((3, rows * Y, X), F32),
-            pltpu.VMEM((2 * height, 2 * BLOCK), F32),
-            pltpu.VMEM((2 * height, 2 * BLOCK), F32),
+            pltpu.VMEM(shifted.shape, F32),
+            pltpu.VMEM((height, 2 * LANES), F32),
+            pltpu.VMEM((height, 2 * LANES), F32),
         ],
-        compiler_params=vmem_mib(20),
+        compiler_params=vmem_mib(18),
         name="backward",
-    )(ext, pred, target, first, second)
+    )(shifted, hidden, pred, target, second)
 
 
 def finish_kernel(one_ref, two_ref, loss_ref, w1_ref, b1_ref, w2_ref, b2_ref):
@@ -523,7 +560,8 @@
         ],
         axis=1,
     )
-    sent = pack(jnp.cos(angles), jnp.sin(angles), sinogram, group, depth)
+    first, second, turned = weights(params)
+    sent = pack(angles, sinogram, group, depth)
     groups = [list(range(s * group, (s + 1) * group)) for s in range(n_sub)]
     got = lax.all_to_all(sent, BOTH, 0, 0, axis_index_groups=groups)
     got = got.reshape(group * local_views, depth + 2 * HALO, DW)
@@ -536,8 +574,8 @@
         others = arrived if others is None else others + arrived
     target = others if n_sub == 2 else others / (n_sub - 1)
 
-    pred, first, second = forward(ext, params)
-    partial = backward(ext, pred, target, first, second, cells)
+    pred, again, shifted, hidden = forward(ext, params, first, turned)
+    partial, target = backward(shifted, hidden, again, target, second, cells)
     loss, grad_w1, grad_b1, grad_w2, grad_b2 = sum_everywhere(partial, channels)
     return (
         pred[None],

time: 74.6 us -> 67.6 us (0.906)
  local copies, waits for them, and re-layouts: 4.84 us -> 1.56 us
  Pallas kernels: 25.2 us -> 22.5 us
  waiting for transfers between devices: 31.6 us -> 30.7 us
    unnamed x11 -> x0, local copies, waits for them, and re-layouts: 3.97 us -> none
    pallas_call x2 -> x3, Pallas kernels: 14.5 us -> 10.7 us  [the longest x1 5.01 us: backward(): pl.pallas_call(functools.partial(backward_kernel, cells), out_shape=(jax....]
    pallas_call x1, Pallas kernels: 1.63 us -> 2.71 us  [pack(): pl.pallas_call(functools.partial(pack_kernel, depth), out_shape=jax.Shape...]
    all_to_all x1, waiting for transfers between devices: 16.3 us -> 15.3 us  [body(): got = lax.all_to_all(sent, BOTH, 0, 0, axis_index_groups=groups)]
  transfers between devices with their start and end apart: 7 -> 7, of which waited for: 6 -> 6; matrix products, arithmetic and copies ran while one was open for 0% -> 2% of each run, Pallas kernels for 8% -> 9%
where the time goes in v2:
time: 67.6 us; the launch traced here: 67.3 us
  waiting for transfers between devices  30.7 us (45%)
  Pallas kernels  22.5 us (33%)
  starting transfers between devices  11.2 us (17%)
  local copies, waits for them, and re-layouts  1.56 us (2%)
  between operations  1.34 us (2%)
    all_to_all x1, waiting for transfers between devices, body(): got = lax.all_to_all(sent, BOTH, 0, 0, axis_index_groups=groups)  15.3 us
    ppermute x5, waiting for transfers between devices, sum_everywhere(): lax.ppermute(value, BOTH, [(i, i ^ apart) for i in range(devices)])  15.3 us
    pallas_call x1, Pallas kernels, project(): pl.pallas_call(functools.partial(project_kernel, scale), out_shape=(jax.S...  8.39 us
    all_to_all x1, starting transfers between devices, body(): got = lax.all_to_all(sent, BOTH, 0, 0, axis_index_groups=groups)  7.43 us
    pallas_call x1, Pallas kernels, backward(): pl.pallas_call(functools.partial(backward_kernel, cells), out_shape=(jax....  5.01 us
    pallas_call x1, Pallas kernels, forward(): pl.pallas_call(forward_kernel, out_shape=(own, own, jax.ShapeDtypeStruct(...  4.8 us
    pallas_call x1, Pallas kernels, pack(): pl.pallas_call(functools.partial(pack_kernel, depth), out_shape=jax.Shape...  2.71 us
    ppermute x5, starting transfers between devices, sum_everywhere(): lax.ppermute(value, BOTH, [(i, i ^ apart) for i in range(devices)])  2.19 us
  transfers between devices with their start and end apart: 7, of which 6 were waited for; matrix products, arithmetic and copies ran while one was open for 2% of the time, Pallas kernels for 9%

profile of v2, /device:TPU:0, one launch (start us, length us, event | category | flops | bytes accessed | tf_op | source)
XLA Modules:
  0.0 67.3 jit_solution(12109363336681442074)
XLA Ops:
  0.6 2.7 %pack.1 = bf16[16,2,8,1280]{3,2,1,0:T(8,128)(2,1)} custom-call(f32[2]{0:T(128)} %angle_ref.1, bf16[2,64,2048]{2,1,0:T(8,128)(2,1)} %sino_ref.1), custom_call_target="tpu_custom_call" | custom-call | tf_op jit(solution)/shard_map/pack/pallas_call | solution.py:93
  3.4 7.4 %all-to-all-start = ((bf16[16,2,8,1280]{3,2,1,0:T(8,128)(2,1)}), bf16[16,2,8,1280]{3,2,1,0:T(8,128)(2,1)S(1)}, u32[]{:S(2)}, u32[]{:S(2)}) async-start(bf16[16,2,8,1280]{3,2,1,0:T(8,128)(2,1)} %pack.1), calls=%async_computation | async-start | bytes 1310720 | tf_op jit(solution)/shard_map/all_to_all | solution.py:566
  11.4 0.7 %copy.13 = f32[32,1]{1,0:T(8,128)S(1)} copy(f32[32,1]{0,1:T(1,128)} %bitcast.10) | data formatting | bytes 256 | tf_op jit(solution)/shard_map/broadcast_in_dim | solution.py:556
  12.2 0.8 %concatenate.3.params_ref = f32[32,128]{1,0:T(8,128)S(1)} concatenate(f32[32,27]{1,0:T(8,128)} %param.8, f32[32,1]{1,0:T(8,128)S(1)} %copy.13, f32[32,4]{1,0:T(8,128)S(1)} %broadcast_in_dim.18, f32[32,27]{1,0:T(8,128)} %param.10, f32[32,69]{1,0:T(8,128)S(1)} %broadcast_in_dim.19), dimensions={1} | concatenate | bytes 32768 | tf_op jit(solution)/shard_map/concatenate | solution.py:553
  13.0 0.9 %weights.1 = (bf16[256,256]{1,0:T(8,128)(2,1)S(1)}, bf16[256,256]{1,0:T(8,128)(2,1)S(1)}, bf16[256,256]{1,0:T(8,128)(2,1)S(1)}) custom-call(f32[32,128]{1,0:T(8,128)S(1)} %concatenate.3.params_ref), custom_call_target="tpu_custom_call" | custom-call | tf_op jit(solution)/shard_map/weights/pallas_call | solution.py:343
  13.9 15.3 %all-to-all-done = bf16[16,2,8,1280]{3,2,1,0:T(8,128)(2,1)S(1)} async-done(((bf16[16,2,8,1280]{3,2,1,0:T(8,128)(2,1)}), bf16[16,2,8,1280]{3,2,1,0:T(8,128)(2,1)S(1)}, u32[]{:S(2)}, u32[]{:S(2)}) %all-to-all-start) | async-done | bytes 655392 | tf_op jit(solution)/shard_map/all_to_all | solution.py:566
  29.3 8.4 %project.1 = (f32[8,8,1024]{2,1,0:T(8,128)S(1)}, f32[4,8,1024]{2,1,0:T(8,128)S(1)}) custom-call(bf16[32,8,1280]{2,1,0:T(8,128)(2,1)S(1)} %bitcast.9), custom_call_target="tpu_custom_call" | custom-call | tf_op jit(solution)/shard_map/project/pallas_call | solution.py:207
  37.7 1.6 %collective-permute-start = (f32[4,8,1024]{2,1,0:T(8,128)S(1)}, f32[4,8,1024]{2,1,0:T(8,128)S(1)}, u32[]{:S(2)}, u32[]{:S(2)}) collective-permute-start(f32[4,8,1024]{2,1,0:T(8,128)S(1)} %get-tuple-element.30), channel_id=1, source_target_pairs={{0,16},{1,17},{2,18},{3,19},{4,20},{5,21},{6,22},{7,23},{8,24},{9,... | collective-permute-start | bytes 393224 | tf_op jit(solution)/shard_map/ppermute | solution.py:573
  39.2 4.8 %forward.1 = (f32[4,8,1024]{2,1,0:T(8,128)}, f32[4,8,1024]{2,1,0:T(8,128)S(1)}, f32[3,64,1024]{2,1,0:T(8,128)S(1)}, bf16[1536,1024]{1,0:T(8,128)(2,1)S(1)}) custom-call(f32[8,8,1024]{2,1,0:T(8,128)S(1)} %get-tuple-element.23.ext_ref, f32[32,128]{1,0:T(8,128)S(1)} %concatenate.3.params_ref, bf16[256,256]{1,0:T(8,128)(2,1)S(1)} %get-tuple-element.24.first_ref, ...), custom_call_target="tpu_custom_call" | custom-call | flops 20000000000 | bytes 2000000 | tf_op jit(solution)/shard_map/forward/pallas_call | solution.py:399
  44.0 0.0 collective-permute-done.target_ref
  44.0 5.0 %backward.1 = (f32[40,128]{1,0:T(8,128)S(1)}, f32[4,8,1024]{2,1,0:T(8,128)}) custom-call(f32[3,64,1024]{2,1,0:T(8,128)S(1)} %get-tuple-element.27.shifted_ref, bf16[1536,1024]{1,0:T(8,128)(2,1)S(1)} %get-tuple-element.28.hidden_ref, f32[4,8,1024]{2,1,0:T(8,128)S(1)} %get-tuple-element.29.pred_ref, f32[4,8,1024]{2,1,0:T(8,128)S(1)} %collective-permute-done.target_ref, ...), custom_call_target="tpu_custom_call" | custom-call | tf_op jit(solution)/shard_map/backward/pallas_call | solution.py:492
  49.1 0.6 collective-permute-start.1
  49.7 3.2 %collective-permute-done.1 = f32[40,128]{1,0:T(8,128)S(1)} collective-permute-done((f32[40,128]{1,0:T(8,128)S(1)}, f32[40,128]{1,0:T(8,128)S(1)}, u32[]{:S(2)}, u32[]{:S(2)}) %collective-permute-start.1) | collective-permute-done | bytes 20512 | tf_op jit(solution)/shard_map/ppermute | solution.py:525
  52.9 1.0 %collective-permute-start.2 = (f32[40,128]{1,0:T(8,128)S(1)}, f32[40,128]{1,0:T(8,128)S(1)}, u32[]{:S(2)}, u32[]{:S(2)}) collective-permute-start(f32[40,128]{1,0:T(8,128)S(1)} %add.12), channel_id=1, source_target_pairs={{0,2},{1,3},{2,0},{3,1},{4,6},{5,7},{6,4},{7,5},{8,10},{9,11},{10,... | collective-permute-start | bytes 61448 | tf_op jit(solution)/shard_map/ppermute | solution.py:525
  53.9 3.0 %collective-permute-done.2 = f32[40,128]{1,0:T(8,128)S(1)} collective-permute-done((f32[40,128]{1,0:T(8,128)S(1)}, f32[40,128]{1,0:T(8,128)S(1)}, u32[]{:S(2)}, u32[]{:S(2)}) %collective-permute-start.2) | collective-permute-done | bytes 20512 | tf_op jit(solution)/shard_map/ppermute | solution.py:525
  56.9 0.0 collective-permute-start.3
  56.9 4.7 %collective-permute-done.3 = f32[40,128]{1,0:T(8,128)S(1)} collective-permute-done((f32[40,128]{1,0:T(8,128)S(1)}, f32[40,128]{1,0:T(8,128)S(1)}, u32[]{:S(2)}, u32[]{:S(2)}) %collective-permute-start.3) | collective-permute-done | bytes 20512 | tf_op jit(solution)/shard_map/ppermute | solution.py:525
  61.6 0.0 collective-permute-start.4
  61.6 1.2 %collective-permute-done.4 = f32[40,128]{1,0:T(8,128)S(1)} collective-permute-done((f32[40,128]{1,0:T(8,128)S(1)}, f32[40,128]{1,0:T(8,128)S(1)}, u32[]{:S(2)}, u32[]{:S(2)}) %collective-permute-start.4) | collective-permute-done | bytes 20512 | tf_op jit(solution)/shard_map/ppermute | solution.py:525
  62.8 0.5 collective-permute-start.5
  63.3 3.2 %collective-permute-done.5.two_ref = f32[40,128]{1,0:T(8,128)S(1)} collective-permute-done((f32[40,128]{1,0:T(8,128)S(1)}, f32[40,128]{1,0:T(8,128)S(1)}, u32[]{:S(2)}, u32[]{:S(2)}) %collective-permute-start.5) | collective-permute-done | bytes 20512 | tf_op jit(solution)/shard_map/ppermute | solution.py:525
  66.6 0.7 %finish.1 = (f32[1,1]{1,0:T(1,128)}, f32[32,27]{1,0:T(8,128)}, f32[1,32]{1,0:T(1,128)}, f32[32,27]{1,0:T(8,128)}, f32[1,1]{1,0:T(1,128)}) custom-call(f32[40,128]{1,0:T(8,128)S(1)} %add.15.one_ref, f32[40,128]{1,0:T(8,128)S(1)} %collective-permute-done.5.two_ref), custom_call_target="tpu_custom_call" | custom-call | tf_op jit(solution)/shard_map/finish/pallas_call | solution.py:531
  (6 shorter events, 0.0 us)
Async XLA Ops:
  3.4 25.9 %all-to-all-start = ((bf16[16,2,8,1280]{3,2,1,0:T(8,128)(2,1)}), bf16[16,2,8,1280]{3,2,1,0:T(8,128)(2,1)S(1)}, u32[]{:S(2)}, u32[]{:S(2)}) async-start(bf16[16,2,8,1280]{3,2,1,0:T(8,128)(2,1)} %pack.1), calls=%async_computation | async-start | bytes 1310720 | tf_op jit(solution)/shard_map/all_to_all | solution.py:566
  37.7 6.4 %collective-permute-start = (f32[4,8,1024]{2,1,0:T(8,128)S(1)}, f32[4,8,1024]{2,1,0:T(8,128)S(1)}, u32[]{:S(2)}, u32[]{:S(2)}) collective-permute-start(f32[4,8,1024]{2,1,0:T(8,128)S(1)} %get-tuple-element.30), channel_id=1, source_target_pairs={{0,16},{1,17},{2,18},{3,19},{4,20},{5,21},{6,22},{7,23},{8,24},{9,... | collective-permute-start | bytes 393224 | tf_op jit(solution)/shard_map/ppermute | solution.py:573
  49.1 3.8 %collective-permute-start.1 = (f32[40,128]{1,0:T(8,128)S(1)}, f32[40,128]{1,0:T(8,128)S(1)}, u32[]{:S(2)}, u32[]{:S(2)}) collective-permute-start(f32[40,128]{1,0:T(8,128)S(1)} %get-tuple-element.33), channel_id=1, source_target_pairs={{0,1},{1,0},{2,3},{3,2},{4,5},{5,4},{6,7},{7,6},{8,9},{9,8},{10,11... | collective-permute-start | bytes 61448 | tf_op jit(solution)/shard_map/ppermute | solution.py:525
  52.9 4.0 %collective-permute-start.2 = (f32[40,128]{1,0:T(8,128)S(1)}, f32[40,128]{1,0:T(8,128)S(1)}, u32[]{:S(2)}, u32[]{:S(2)}) collective-permute-start(f32[40,128]{1,0:T(8,128)S(1)} %add.12), channel_id=1, source_target_pairs={{0,2},{1,3},{2,0},{3,1},{4,6},{5,7},{6,4},{7,5},{8,10},{9,11},{10,... | collective-permute-start | bytes 61448 | tf_op jit(solution)/shard_map/ppermute | solution.py:525
  56.9 4.7 %collective-permute-start.3 = (f32[40,128]{1,0:T(8,128)S(1)}, f32[40,128]{1,0:T(8,128)S(1)}, u32[]{:S(2)}, u32[]{:S(2)}) collective-permute-start(f32[40,128]{1,0:T(8,128)S(1)} %add.13), channel_id=1, source_target_pairs={{0,4},{1,5},{2,6},{3,7},{4,0},{5,1},{6,2},{7,3},{8,12},{9,13},{10,... | collective-permute-start | bytes 61448 | tf_op jit(solution)/shard_map/ppermute | solution.py:525
  61.6 1.2 %collective-permute-start.4 = (f32[40,128]{1,0:T(8,128)S(1)}, f32[40,128]{1,0:T(8,128)S(1)}, u32[]{:S(2)}, u32[]{:S(2)}) collective-permute-start(f32[40,128]{1,0:T(8,128)S(1)} %add.14), channel_id=1, source_target_pairs={{0,8},{1,9},{2,10},{3,11},{4,12},{5,13},{6,14},{7,15},{8,0},{9,1},... | collective-permute-start | bytes 61448 | tf_op jit(solution)/shard_map/ppermute | solution.py:525
  62.8 3.8 %collective-permute-start.5 = (f32[40,128]{1,0:T(8,128)S(1)}, f32[40,128]{1,0:T(8,128)S(1)}, u32[]{:S(2)}, u32[]{:S(2)}) collective-permute-start(f32[40,128]{1,0:T(8,128)S(1)} %add.15.one_ref), channel_id=1, source_target_pairs={{0,16},{1,17},{2,18},{3,19},{4,20},{5,21},{6,22},{7,23},{8,24},{9,... | collective-permute-start | bytes 61448 | tf_op jit(solution)/shard_map/ppermute | solution.py:525
